TPU v7x, 32 devices: a whole 2x2x4 slice. The times are simulated.
32 devices in a mesh: img: 4 (over y, x), proto: 8 (over z, core).
Axes of the slice: x: 2, y: 2, z: 4, core: 2. Of those that a mesh axis runs over, the one named last changes fastest.
Arguments:
- student_patch_tokens: bfloat16 [4, 256, 4096], P('img', None, 'proto'), may hold values from -6 to 6
- teacher_patch_tokens: bfloat16 [4, 256, 4096], P('img', None, 'proto'), may hold values from -6 to 6
- mask_counts: int32 [4], P('img'), may hold values from 32 to 128, as said below
- mask_index: int32 [4, 128], P('img'), may hold values from 0 to 255, as said below
- student_bottleneck: bfloat16 [4096, 256], P('proto'), may hold values from -0.09375 to 0.09375
- teacher_bottleneck: bfloat16 [4096, 256], P('proto'), may hold values from -0.09375 to 0.09375
- student_protos: bfloat16 [256, 98304], P(None, 'proto'), may hold values from -60 to 60
- teacher_protos: bfloat16 [256, 98304], P(None, 'proto'), may hold values from -60 to 60
- center: float32 [98304], P('proto'), may hold values from -0.75 to 0.75
Outputs:
- image_loss: float32 [4], P('img')
- grad_protos: float32 [256, 98304], P('img', 'proto')
- grad_bottleneck: float32 [4096, 256], P('proto', 'img')
Inputs may be any that keep to these rules, and one draw needn't show every extreme that they name: `mask_counts`: some image has exactly 128 masked patches. `mask_index`: the 128 entries of an image are distinct patch numbers; only the first mask_counts of them are used.
All inputs are finite; a program needn't handle non-finite values.
Results may differ from a plain program's by a relative error of at most 0.0071.
Values may be sent and summed in bfloat16 or wider, within the bound.
No kernel may reach another device: no remote copies, remote signals or barrier semaphores. Data moves between devices by JAX's collectives and lax.ppermute only.
A program may use at most 64 MiB of HBM per device.

v0:
```python
import jax
import jax.numpy as jnp
from jax import lax
from jax.sharding import PartitionSpec as P

EPSILON = 1e-06
STUDENT_TEMP = 0.1
TEACHER_TEMP = 0.04
LOSS_SCALE = 4096.0


def scores(units_student, units_teacher, weight, student_protos, teacher_protos, center):
    logits_student = (
        jnp.dot(units_student, student_protos, preferred_element_type=jnp.float32) / STUDENT_TEMP
    )
    logits_teacher = (
        jnp.dot(units_teacher, teacher_protos, preferred_element_type=jnp.float32) - center[None, :]
    ) / TEACHER_TEMP
    top_student, top_teacher = lax.pmax(
        (jnp.max(logits_student, axis=1), jnp.max(logits_teacher, axis=1)), "proto"
    )
    exp_student = jnp.exp(logits_student - top_student[:, None])
    exp_teacher = jnp.exp(logits_teacher - top_teacher[:, None])
    total_student, total_teacher, cross = lax.psum(
        (
            jnp.sum(exp_student, axis=1),
            jnp.sum(exp_teacher, axis=1),
            jnp.sum(exp_teacher * logits_student, axis=1),
        ),
        "proto",
    )
    loss_rows = -(cross / total_teacher - top_student - jnp.log(total_student))
    differ = exp_student / total_student[:, None] - exp_teacher / total_teacher[:, None]
    logit_gradient = (
        LOSS_SCALE * weight.astype(jnp.float32)[:, None] * differ / STUDENT_TEMP
    ).astype(jnp.bfloat16)
    return (loss_rows, logit_gradient)


def prototype_gradient(row_units, logit_gradient):
    return lax.psum_scatter(
        lax.dot_general(
            row_units, logit_gradient, (((0,), (0,)), ((), ())), preferred_element_type=jnp.float32
        ),
        "img",
        scatter_dimension=0,
        tiled=True,
    )


def per_device(
    student_patch_tokens,
    teacher_patch_tokens,
    mask_counts,
    mask_index,
    student_bottleneck,
    teacher_bottleneck,
    student_protos,
    teacher_protos,
    center,
):
    img_local, patch_total, width_local = student_patch_tokens.shape
    mask_width = mask_index.shape[1]
    rows_local = img_local * mask_width
    patch_iota = lax.broadcasted_iota(jnp.int32, (img_local, mask_width, patch_total), 2)
    masked_picker = (mask_index[:, :, None] == patch_iota).astype(jnp.bfloat16)
    student_token_rows = (
        jnp.einsum(
            "oaz,oze->oae", masked_picker, student_patch_tokens, preferred_element_type=jnp.float32
        )
        .astype(jnp.bfloat16)
        .reshape(rows_local, width_local)
    )
    teacher_rows = (
        jnp.einsum(
            "oaz,oze->oae", masked_picker, teacher_patch_tokens, preferred_element_type=jnp.float32
        )
        .astype(jnp.bfloat16)
        .reshape(rows_local, width_local)
    )
    partial_student = jnp.dot(
        student_token_rows, student_bottleneck, preferred_element_type=jnp.float32
    )
    partial_teacher = jnp.dot(teacher_rows, teacher_bottleneck, preferred_element_type=jnp.float32)
    hidden_student, hidden_teacher = lax.psum((partial_student, partial_teacher), "proto")
    inv_student = lax.rsqrt(
        jnp.sum(hidden_student * hidden_student, axis=1, keepdims=True) + EPSILON
    )
    inv_teacher = lax.rsqrt(
        jnp.sum(hidden_teacher * hidden_teacher, axis=1, keepdims=True) + EPSILON
    )
    units_student = (hidden_student * inv_student).astype(jnp.bfloat16)
    units_teacher = (hidden_teacher * inv_teacher).astype(jnp.bfloat16)
    position = lax.broadcasted_iota(jnp.int32, (img_local, mask_width), 1)
    live_grid = position < mask_counts[:, None]
    weight = (
        jnp.where(live_grid, 1.0 / mask_counts.astype(jnp.float32)[:, None], 0.0)
        .astype(jnp.bfloat16)
        .reshape(rows_local)
    )
    loss_rows, logit_gradient = scores(
        units_student, units_teacher, weight, student_protos, teacher_protos, center
    )
    weighted = weight.astype(jnp.float32) * loss_rows
    image_loss = jnp.sum(weighted.reshape(img_local, mask_width), axis=1)
    grad_protos = prototype_gradient(units_student, logit_gradient)
    partial_rows = lax.dot_general(
        logit_gradient, student_protos, (((1,), (1,)), ((), ())), preferred_element_type=jnp.float32
    )
    grad_rows = lax.psum(partial_rows, "proto")
    inner = jnp.sum(hidden_student * grad_rows, axis=1, keepdims=True)
    grad_hidden = (
        grad_rows * inv_student - hidden_student * inner * (inv_student * inv_student * inv_student)
    ).astype(jnp.bfloat16)
    local_term = lax.dot_general(
        student_token_rows,
        grad_hidden,
        (((0,), (0,)), ((), ())),
        preferred_element_type=jnp.float32,
    )
    grad_bottleneck = lax.psum_scatter(local_term, "img", scatter_dimension=1, tiled=True)
    return (image_loss, grad_protos, grad_bottleneck)


def solution(mesh):
    placed = (
        P("img", None, "proto"),
        P("img", None, "proto"),
        P("img"),
        P("img", None),
        P("proto", None),
        P("proto", None),
        P(None, "proto"),
        P(None, "proto"),
        P("proto"),
    )
    return jax.shard_map(
        per_device,
        mesh=mesh,
        in_specs=placed,
        out_specs=(P("img"), P("img", "proto"), P("proto", "img")),
        check_vma=False,
    )
```

profile of v0, /device:TPU:0, one launch (start us, length us, event | category | flops | bytes accessed | tf_op | source)
XLA Modules:
  0.0 341.4 jit_solution(12172484744703447159)
XLA Ops:
  7.2 0.9 copy-done
  8.1 0.9 convolution_convert_fusion
  9.0 0.6 copy-done.2
  9.7 1.8 fusion.25
  11.5 2.1 fusion.3
  13.5 0.0 all-reduce.6.cloned.1.call-start
  14.3 57.6 %all-reduce.8.cloned.1.call-done = (f32[128,256]{1,0:T(8,128)}, f32[128,256]{1,0:T(8,128)}) async-done(((f32[128,256]{1,0:T(8,128)}, f32[128,256]{1,0:T(8,128)}), (f32[128,256]{1,0:T(8,128)}, f32[128,256]{1,0:T(8,128)})) %all-reduce.8.cloned.1.call-update) | async-done | bytes 262160 | tf_op jit(solution)/shard_map/psum | solution.py:85
  71.9 1.2 multiply_reduce_fusion.2
  73.2 0.5 multiply_multiply_fusion
  73.7 6.7 %fusion.24 = (f32[128]{0:T(128)S(1)}, f32[128,12288]{1,0:T(8,128)}) fusion(bf16[256,12288]{1,0:T(8,128)(2,1)} %param.15, f32[128,256]{1,0:T(8,128)} %get-tuple-element.10, f32[128]{0:T(128)S(1)} %get-tuple-element.14), kind=kOutput, calls=%fused_computation.39 | convolution fusion | flops 808517504 | bytes 12715008 | tf_op jit(solution)/shard_map/dot_general | solution.py:14
  80.5 4.0 %fusion.23 = (f32[128]{0:T(128)S(1)}, f32[128,12288]{1,0:T(8,128)}) fusion(f32[12288]{0:T(1024)S(1)} %copy-done.4, bf16[256,12288]{1,0:T(8,128)(2,1)S(1)} %bitcast.28, f32[128,256]{1,0:T(8,128)S(1)} %copy-done.3, f32[128]{0:T(128)S(1)} %add_rsqrt_fusion.1), kind=kOutput, calls=%fused_computation.38 | convolution fusion | flops 810090368 | bytes 12764160 | tf_op jit(solution)/shard_map/dot_general | solution.py:17
  84.5 13.7 %all-reduce.2 = (f32[128]{0:T(128)S(1)}, f32[128]{0:T(128)S(1)}) all-reduce(f32[128]{0:T(128)S(1)} %get-tuple-element.15, f32[128]{0:T(128)S(1)} %get-tuple-element.17), channel_id=1, replica_groups=mesh['img'=4,'proto'=8] {'proto'}, use_global_device_ids=true, to_apply=%region_3.0 | all-reduce | flops 256 | bytes 2048 | tf_op jit(solution)/shard_map/pmax | solution.py:19
  98.1 5.9 %fusion.2 = (f32[128]{0:T(128)S(1)}, f32[128]{0:T(128)S(1)}, f32[128]{0:T(128)S(1)}) fusion(f32[128,12288]{1,0:T(8,128)} %get-tuple-element.16, f32[128]{0:T(128)S(1)} %get-tuple-element.11, f32[128,12288]{1,0:T(8,128)} %get-tuple-element.18, f32[128]{0:T(128)S(1)} %get-tuple-element.12), kind=kLoop, calls=%fused_computation.8 | loop fusion | flops 9436800 | bytes 12585472 | tf_op jit(solution)/shard_map/reduce_sum | solution.py:27
  104.0 14.1 %all-reduce = (f32[128]{0:T(128)S(1)}, f32[128]{0:T(128)}, f32[128]{0:T(128)S(1)}) all-reduce(f32[128]{0:T(128)S(1)} %get-tuple-element.5, f32[128]{0:T(128)S(1)} %get-tuple-element.4, f32[128]{0:T(128)S(1)} %get-tuple-element.3), channel_id=1, replica_groups=mesh['img'=4,'proto'=8] {'proto'}, use_global_device_ids=true, to_apply=%region_13.14 | all-reduce | flops 384 | bytes 3072 | tf_op jit(solution)/shard_map/psum | solution.py:24
  118.2 5.9 %multiply_convert_fusion = bf16[128,12288]{1,0:T(8,128)(2,1)S(1)} fusion(f32[128,12288]{1,0:T(8,128)} %get-tuple-element.18, f32[128,12288]{1,0:T(8,128)} %get-tuple-element.16, f32[128]{0:T(128)S(1)} %get-tuple-element.8, f32[128]{0:T(128)S(1)} %get-tuple-element.6, f32[128]{0:T(128)S(1)} %fusion.21, f32[128]{0:T(128)S(1)} %get-tuple-element.12, ...), kind=kLoop, calls=%fused_computation.3 | loop fusion | flops 12582912 | bytes 15731200 | tf_op jit(solution)/shard_map/convert_element_type | solution.py:36
  124.1 5.7 %fusion.26 = f32[128,256]{1,0:T(8,128)} fusion(bf16[128,12288]{1,0:T(8,128)(2,1)S(1)} %multiply_convert_fusion, bf16[256,12288]{1,0:T(8,128)(2,1)} %param.15), kind=kOutput, calls=%fused_computation.41 | convolution fusion | flops 805306368 | bytes 9568256 | tf_op jit(solution)/shard_map/dot_general | solution.py:107
  129.9 53.2 %all-reduce.6.cloned.1.call-done = f32[128,256]{1,0:T(8,128)} async-done(((f32[128,256]{1,0:T(8,128)}), f32[128,256]{1,0:T(8,128)}) %all-reduce.6.cloned.1.call-update) | async-done | bytes 131088 | tf_op jit(solution)/shard_map/psum | solution.py:110
  183.1 1.0 multiply_reduce_fusion.1
  184.2 2.2 fusion.11
  186.4 6.5 %fusion.22 = f32[256,12288]{1,0:T(8,128)} fusion(bf16[128,12288]{1,0:T(8,128)(2,1)S(1)} %multiply_convert_fusion, f32[128,256]{1,0:T(8,128)S(1)} %copy-done.1, f32[128]{0:T(128)S(1)} %get-tuple-element.14), kind=kOutput, calls=%fused_computation.37 | convolution fusion | flops 805371904 | bytes 15860224 | tf_op jit(solution)/shard_map/dot_general | solution.py:42
  192.9 0.6 copy-done.5
  193.5 0.6 multiply_reduce_fusion.4
  194.1 16.6 %reduce-scatter.5.cloned.1.call-done = f32[512,64]{0,1:T(8,128)} async-done(((f32[512,256]{0,1:T(8,128)}), f32[512,64]{0,1:T(8,128)}) %reduce-scatter.5.cloned.1.call-update) | async-done | bytes 131088 | tf_op jit(solution)/shard_map/reduce_scatter | solution.py:121
  210.7 124.2 %reduce-scatter.3.cloned.1.call-done = f32[64,12288]{1,0:T(8,128)} async-done(((f32[256,12288]{1,0:T(8,128)}), f32[64,12288]{1,0:T(8,128)}) %reduce-scatter.3.cloned.1.call-update) | async-done | bytes 3145744 | tf_op jit(solution)/shard_map/reduce_scatter | solution.py:41
  (23 shorter events, 0.2 us)
Async XLA Ops:
  7.2 1.0 copy-start
  7.2 64.8 %all-reduce.8.cloned.1.call-start = ((), (), s32[]{:S(2)}) async-start(), calls=%async_computation.5 | async-start | bytes 524288 | tf_op jit(solution)/shard_map/psum | solution.py:85
  9.0 0.7 copy-start.2
  13.5 169.6 %all-reduce.6.cloned.1.call-start = ((), (), s32[]{:S(2)}) async-start(), calls=%async_computation.3 | async-start | bytes 262144 | tf_op jit(solution)/shard_map/psum | solution.py:110
  71.9 8.5 %slice-start = ((s8[6291456]{0:T(1024)(128)(4,1)}), s8[4194304]{0:T(1024)(128)(4,1)S(1)}, s32[]{:S(2)}) async-start(s8[6291456]{0:T(1024)(128)(4,1)} %bitcast.27), calls=%async_computation.6 | async-start | bytes 8388608
  73.7 6.8 %slice-start.1 = ((s8[6291456]{0:T(1024)(128)(4,1)}), s8[2097152]{0:T(1024)(128)(4,1)S(1)}, s32[]{:S(2)}) async-start(s8[6291456]{0:T(1024)(128)(4,1)} %bitcast.27), calls=%async_computation.7 | async-start | bytes 4194304
  73.7 6.8 %copy-start.3 = (f32[128,256]{1,0:T(8,128)S(1)}, f32[128,256]{1,0:T(8,128)}, u32[]{:S(2)}) copy-start(f32[128,256]{1,0:T(8,128)} %get-tuple-element.9) | copy-start | bytes 393220
  73.7 6.8 %copy-start.4 = (f32[12288]{0:T(1024)S(1)}, f32[12288]{0:T(1024)}, u32[]{:S(2)}) copy-start(f32[12288]{0:T(1024)} %param.17) | copy-start | bytes 147460
  124.1 59.0 %copy-start.1 = (f32[128,256]{1,0:T(8,128)S(1)}, f32[128,256]{1,0:T(8,128)}, u32[]{:S(2)}) copy-start(f32[128,256]{1,0:T(8,128)} %get-tuple-element.10) | copy-start | bytes 393220
  129.9 80.9 %reduce-scatter.5.cloned.1.call-start = ((), (), s32[]{:S(2)}) async-start(), calls=%async_computation.4 | async-start | bytes 655360 | tf_op jit(solution)/shard_map/reduce_scatter | solution.py:121
  186.3 148.5 %reduce-scatter.3.cloned.1.call-start = ((), (), s32[]{:S(2)}) async-start(), calls=%async_computation.2 | async-start | bytes 15728640 | tf_op jit(solution)/shard_map/reduce_scatter | solution.py:41
  192.8 0.6 copy-start.5
Sparse Core Ops, SparseCore 0:
  13.7 58.2 all-reduce.7
  130.0 53.1 all-reduce.5
  186.5 24.1 reduce-scatter.4
  214.2 120.5 reduce-scatter.2
where the time goes:
time: 342 us; the launch traced here: 341 us
  waiting for transfers between devices  252 us (74%)
  matrix products  29.8 us (9%)
  blocking collectives  27.8 us (8%)
  other arithmetic  15.2 us (4%)
  between operations  14.5 us (4%)
    reduce_scatter x1, waiting for transfers between devices, prototype_gradient(): lax.psum_scatter(lax.dot_general(row_units, logit_gradient, (((0,), (0,))...  124 us
    psum x1, waiting for transfers between devices, per_device(): lax.psum((partial_student, partial_teacher), 'proto')  57.6 us
    psum x1, waiting for transfers between devices, per_device(): grad_rows = lax.psum(partial_rows, 'proto')  53.2 us
    reduce_scatter x1, waiting for transfers between devices, per_device(): lax.psum_scatter(local_term, 'img', scatter_dimension=1, tiled=True)  16.6 us
    psum x1, blocking collectives, scores(): lax.psum((jnp.sum(exp_student, axis=1), jnp.sum(exp_teacher, axis=1), jnp...  14.1 us
    pmax x1, blocking collectives, scores(): lax.pmax((jnp.max(logits_student, axis=1), jnp.max(logits_teacher, axis=1...  13.7 us
  transfers between devices with their start and end apart: 4, of which 4 were waited for; matrix products, arithmetic and copies ran while one was open for 2% of the time, Pallas kernels for 0%

commit v1 on v0

--- a/solution.py
+++ b/solution.py
@@ -107,7 +107,7 @@
     partial_rows = lax.dot_general(
         logit_gradient, student_protos, (((1,), (1,)), ((), ())), preferred_element_type=jnp.float32
     )
-    grad_rows = lax.psum(partial_rows, "proto")
+    grad_rows = jnp.sum(lax.all_gather(partial_rows, "proto"), axis=0)
     inner = jnp.sum(hidden_student * grad_rows, axis=1, keepdims=True)
     grad_hidden = (
         grad_rows * inv_student - hidden_student * inner * (inv_student * inv_student * inv_student)

time: 342 us -> 311 us (0.909)
  waiting for transfers between devices: 252 us -> 219 us
    psum x1 -> x0, waiting for transfers between devices: 53.2 us -> none  [per_device(): grad_rows = lax.psum(partial_rows, 'proto')]
    all_gather x0 -> x1, waiting for transfers between devices: none -> 20.5 us  [per_device(): grad_rows = jnp.sum(lax.all_gather(partial_rows, 'proto'), axis=0)]
where the time goes in v1:
time: 311 us
  waiting for transfers between devices  219 us (70%)
  matrix products  29.8 us (10%)
  blocking collectives  27.8 us (9%)
  other arithmetic  17.2 us (6%)
  between operations  14.5 us (5%)
    reduce_scatter x1, waiting for transfers between devices, prototype_gradient(): lax.psum_scatter(lax.dot_general(row_units, logit_gradient, (((0,), (0,))...  124 us
    psum x1, waiting for transfers between devices, per_device(): lax.psum((partial_student, partial_teacher), 'proto')  57.6 us
    all_gather x1, waiting for transfers between devices, per_device(): grad_rows = jnp.sum(lax.all_gather(partial_rows, 'proto'), axis=0)  20.5 us
    reduce_scatter x1, waiting for transfers between devices, per_device(): lax.psum_scatter(local_term, 'img', scatter_dimension=1, tiled=True)  17.1 us
    psum x1, blocking collectives, scores(): lax.psum((jnp.sum(exp_student, axis=1), jnp.sum(exp_teacher, axis=1), jnp...  14.1 us
    pmax x1, blocking collectives, scores(): lax.pmax((jnp.max(logits_student, axis=1), jnp.max(logits_teacher, axis=1...  13.7 us
    dot_general x1, matrix products, scores(): jnp.dot(units_student, student_protos, preferred_element_type=jnp.float32)  6.74 us
    dot_general x1, matrix products, prototype_gradient(): lax.dot_general(row_units, logit_gradient, (((0,), (0,)), ((), ())), pref...  6.46 us
  transfers between devices with their start and end apart: 4, of which 4 were waited for; matrix products, arithmetic and copies ran while one was open for 2% of the time, Pallas kernels for 0%

profile of v1, /device:TPU:0, one launch (start us, length us, event | category | flops | bytes accessed | tf_op | source)
XLA Modules:
  0.0 311.1 jit_solution(4949381856489049071)
XLA Ops:
  7.2 0.9 copy-done
  8.1 0.9 convolution_convert_fusion
  9.0 0.6 copy-done.2
  9.7 1.8 fusion.25
  11.5 2.1 fusion.3
  14.3 57.6 %all-reduce.5.cloned.1.call-done = (f32[128,256]{1,0:T(8,128)}, f32[128,256]{1,0:T(8,128)}) async-done(((f32[128,256]{1,0:T(8,128)}, f32[128,256]{1,0:T(8,128)}), (f32[128,256]{1,0:T(8,128)}, f32[128,256]{1,0:T(8,128)})) %all-reduce.5.cloned.1.call-update) | async-done | bytes 262160 | tf_op jit(solution)/shard_map/psum | solution.py:85
  71.9 1.2 multiply_reduce_fusion.2
  73.2 0.5 multiply_multiply_fusion
  73.7 6.7 %fusion.24 = (f32[128]{0:T(128)S(1)}, f32[128,12288]{1,0:T(8,128)}) fusion(bf16[256,12288]{1,0:T(8,128)(2,1)} %param.15, f32[128,256]{1,0:T(8,128)} %get-tuple-element.10, f32[128]{0:T(128)S(1)} %get-tuple-element.14), kind=kOutput, calls=%fused_computation.39 | convolution fusion | flops 808517504 | bytes 12715008 | tf_op jit(solution)/shard_map/dot_general | solution.py:14
  80.5 4.0 %fusion.23 = (f32[128]{0:T(128)S(1)}, f32[128,12288]{1,0:T(8,128)}) fusion(f32[12288]{0:T(1024)S(1)} %copy-done.4, bf16[256,12288]{1,0:T(8,128)(2,1)S(1)} %bitcast.29, f32[128,256]{1,0:T(8,128)S(1)} %copy-done.3, f32[128]{0:T(128)S(1)} %add_rsqrt_fusion.1), kind=kOutput, calls=%fused_computation.38 | convolution fusion | flops 810090368 | bytes 12764160 | tf_op jit(solution)/shard_map/dot_general | solution.py:17
  84.5 13.7 %all-reduce.2 = (f32[128]{0:T(128)S(1)}, f32[128]{0:T(128)S(1)}) all-reduce(f32[128]{0:T(128)S(1)} %get-tuple-element.15, f32[128]{0:T(128)S(1)} %get-tuple-element.17), channel_id=1, replica_groups=mesh['img'=4,'proto'=8] {'proto'}, use_global_device_ids=true, to_apply=%region_3.0 | all-reduce | flops 256 | bytes 2048 | tf_op jit(solution)/shard_map/pmax | solution.py:19
  98.1 5.9 %fusion.2 = (f32[128]{0:T(128)S(1)}, f32[128]{0:T(128)S(1)}, f32[128]{0:T(128)S(1)}) fusion(f32[128,12288]{1,0:T(8,128)} %get-tuple-element.16, f32[128]{0:T(128)S(1)} %get-tuple-element.11, f32[128,12288]{1,0:T(8,128)} %get-tuple-element.18, f32[128]{0:T(128)S(1)} %get-tuple-element.12), kind=kLoop, calls=%fused_computation.8 | loop fusion | flops 9436800 | bytes 12585472 | tf_op jit(solution)/shard_map/reduce_sum | solution.py:27
  104.0 14.1 %all-reduce = (f32[128]{0:T(128)S(1)}, f32[128]{0:T(128)}, f32[128]{0:T(128)S(1)}) all-reduce(f32[128]{0:T(128)S(1)} %get-tuple-element.5, f32[128]{0:T(128)S(1)} %get-tuple-element.4, f32[128]{0:T(128)S(1)} %get-tuple-element.3), channel_id=1, replica_groups=mesh['img'=4,'proto'=8] {'proto'}, use_global_device_ids=true, to_apply=%region_13.14 | all-reduce | flops 384 | bytes 3072 | tf_op jit(solution)/shard_map/psum | solution.py:24
  118.2 5.9 %multiply_convert_fusion = bf16[128,12288]{1,0:T(8,128)(2,1)S(1)} fusion(f32[128,12288]{1,0:T(8,128)} %get-tuple-element.18, f32[128,12288]{1,0:T(8,128)} %get-tuple-element.16, f32[128]{0:T(128)S(1)} %get-tuple-element.8, f32[128]{0:T(128)S(1)} %get-tuple-element.6, f32[128]{0:T(128)S(1)} %fusion.21, f32[128]{0:T(128)S(1)} %get-tuple-element.12, ...), kind=kLoop, calls=%fused_computation.3 | loop fusion | flops 12582912 | bytes 15731200 | tf_op jit(solution)/shard_map/convert_element_type | solution.py:36
  124.1 5.7 %fusion.26 = f32[128,256]{1,0:T(8,128)} fusion(bf16[128,12288]{1,0:T(8,128)(2,1)S(1)} %multiply_convert_fusion, bf16[256,12288]{1,0:T(8,128)(2,1)} %param.15), kind=kOutput, calls=%fused_computation.41 | convolution fusion | flops 805306368 | bytes 9568256 | tf_op jit(solution)/shard_map/dot_general | solution.py:107
  129.9 20.5 %all-gather.3.cloned.1.call-done = f32[1024,256]{1,0:T(8,128)} async-done(((f32[128,256]{1,0:T(8,128)}), f32[1024,256]{1,0:T(8,128)}) %all-gather.3.cloned.1.call-update) | async-done | bytes 1048592 | tf_op jit(solution)/shard_map/all_gather | solution.py:110
  150.4 2.0 reduce_sum.81
  152.4 1.0 multiply_reduce_fusion.1
  153.4 2.2 fusion.11
  155.6 6.5 %fusion.22 = f32[256,12288]{1,0:T(8,128)} fusion(bf16[128,12288]{1,0:T(8,128)(2,1)S(1)} %multiply_convert_fusion, f32[128,256]{1,0:T(8,128)S(1)} %copy-done.1, f32[128]{0:T(128)S(1)} %get-tuple-element.14), kind=kOutput, calls=%fused_computation.37 | convolution fusion | flops 805371904 | bytes 15860224 | tf_op jit(solution)/shard_map/dot_general | solution.py:42
  162.1 0.6 copy-done.5
  162.7 0.6 multiply_reduce_fusion.4
  163.3 17.1 %reduce-scatter.5.cloned.1.call-done = f32[512,64]{0,1:T(8,128)} async-done(((f32[512,256]{0,1:T(8,128)}), f32[512,64]{0,1:T(8,128)}) %reduce-scatter.5.cloned.1.call-update) | async-done | bytes 131088 | tf_op jit(solution)/shard_map/reduce_scatter | solution.py:121
  180.4 124.2 %reduce-scatter.3.cloned.1.call-done = f32[64,12288]{1,0:T(8,128)} async-done(((f32[256,12288]{1,0:T(8,128)}), f32[64,12288]{1,0:T(8,128)}) %reduce-scatter.3.cloned.1.call-update) | async-done | bytes 3145744 | tf_op jit(solution)/shard_map/reduce_scatter | solution.py:41
  (24 shorter events, 0.3 us)
Async XLA Ops:
  7.2 1.0 copy-start
  7.2 64.8 %all-reduce.5.cloned.1.call-start = ((), (), s32[]{:S(2)}) async-start(), calls=%async_computation.5 | async-start | bytes 524288 | tf_op jit(solution)/shard_map/psum | solution.py:85
  9.0 0.7 copy-start.2
  13.5 136.8 %all-gather.3.cloned.1.call-start = ((), (), s32[]{:S(2)}) async-start(), calls=%async_computation.4 | async-start | bytes 1179648 | tf_op jit(solution)/shard_map/all_gather | solution.py:110
  71.9 8.5 %slice-start = ((s8[6291456]{0:T(1024)(128)(4,1)}), s8[4194304]{0:T(1024)(128)(4,1)S(1)}, s32[]{:S(2)}) async-start(s8[6291456]{0:T(1024)(128)(4,1)} %bitcast.28), calls=%async_computation.6 | async-start | bytes 8388608
  73.7 6.8 %slice-start.1 = ((s8[6291456]{0:T(1024)(128)(4,1)}), s8[2097152]{0:T(1024)(128)(4,1)S(1)}, s32[]{:S(2)}) async-start(s8[6291456]{0:T(1024)(128)(4,1)} %bitcast.28), calls=%async_computation.7 | async-start | bytes 4194304
  73.7 6.8 %copy-start.3 = (f32[128,256]{1,0:T(8,128)S(1)}, f32[128,256]{1,0:T(8,128)}, u32[]{:S(2)}) copy-start(f32[128,256]{1,0:T(8,128)} %get-tuple-element.9) | copy-start | bytes 393220
  73.7 6.8 %copy-start.4 = (f32[12288]{0:T(1024)S(1)}, f32[12288]{0:T(1024)}, u32[]{:S(2)}) copy-start(f32[12288]{0:T(1024)} %param.17) | copy-start | bytes 147460
  124.1 28.2 %copy-start.1 = (f32[128,256]{1,0:T(8,128)S(1)}, f32[128,256]{1,0:T(8,128)}, u32[]{:S(2)}) copy-start(f32[128,256]{1,0:T(8,128)} %get-tuple-element.10) | copy-start | bytes 393220
  129.9 50.5 %reduce-scatter.5.cloned.1.call-start = ((), (), s32[]{:S(2)}) async-start(), calls=%async_computation.3 | async-start | bytes 655360 | tf_op jit(solution)/shard_map/reduce_scatter | solution.py:121
  155.5 149.0 %reduce-scatter.3.cloned.1.call-start = ((), (), s32[]{:S(2)}) async-start(), calls=%async_computation.2 | async-start | bytes 15728640 | tf_op jit(solution)/shard_map/reduce_scatter | solution.py:41
  162.1 0.6 copy-start.5
Sparse Core Ops, SparseCore 0:
  13.7 58.2 all-reduce.4
  130.0 20.3 all-gather.2
  155.7 24.6 reduce-scatter.4
  183.9 120.6 reduce-scatter.2
